TPU v7x, 256 devices: a whole 4x4x8 slice. The times are simulated.
256 devices in a mesh: tm: 32 (over z_lo, x, core), cells: 8 (over y, z_hi).
Axes of the slice: x: 4, y: 4, z: 8 (z_hi: 2, z_lo: 4; z = z_hi * 4 + z_lo), core: 2. Of those that a mesh axis runs over, the one named last changes fastest.
Arguments:
- hist_bin: int32 [16384, 8192], P('tm', 'cells'), may hold values from 0 to 255
- obs_bin: int32 [16384, 8192], P('tm', 'cells'), may hold values from 0 to 255
- fut_bin: int32 [16384, 8192], P('tm', 'cells'), may hold values from 0 to 255
- region_id: int32 [8192], P('cells'), may hold values from 0 to 127, as said below
- bin_width: float32 [8192], P('cells'), may hold values from 0.005 to 0.05
- bin_offset: float32 [8192], P('cells'), may hold values from -4 to 4
Outputs:
- adjusted: float32 [16384, 8192], P('tm', 'cells')
Inputs may be any that keep to these rules, and one draw needn't show every extreme that they name: `region_id`: every zone of 0 to 127 holds exactly 64 cells.
All inputs are finite; a program needn't handle non-finite values.
Results may differ from a plain program's by a relative error of at most 0.0003.
Values sent between devices are 32-bit elements; how exact they have to be, the bound alone decides.
A program may use at most 64 MiB of HBM per device.

v0:
```python
import math
import jax
import jax.numpy as jnp
from jax import lax
from jax.sharding import PartitionSpec as P

BINS = 256
REGIONS = 128
pool_weight = 0.5


def in_order(blocks, dim):
    blocks = jnp.moveaxis(blocks, 0, dim)
    dims = blocks.shape
    return blocks.reshape(*dims[:dim], dims[dim] * dims[dim + 1], *dims[dim + 2 :])


def copy_for_each(array, axis):
    count = lax.axis_size(axis)
    return lax.all_to_all(
        jnp.broadcast_to(array[None], (count, *array.shape)), axis, 0, 0, tiled=True
    )


def collect(array, axis, dim):
    return in_order(copy_for_each(array, axis), dim)


def tally_bins(stacked, levels):
    series, day_count, cell_count = stacked.shape
    day_block = math.gcd(day_count, max(1, 16384 // cell_count))

    def add_block(turn_index, totals):
        portion = lax.dynamic_slice_in_dim(stacked, turn_index * day_block, day_block, 1)
        matches = (portion[..., None] == levels).astype(jnp.bfloat16)
        return totals + jnp.sum(matches, axis=1, dtype=jnp.float32)

    initial = jnp.zeros((series, cell_count, levels.shape[0]), jnp.float32)
    return lax.fori_loop(0, day_count // day_block, add_block, initial)


def quantile_at(rank_rows, before_rows, pooled_rows):
    ramp_terms = jnp.minimum(
        jnp.maximum(rank_rows[:, :, None] - before_rows[:, None, :], 0.0), pooled_rows[:, None, :]
    )
    return jnp.sum(ramp_terms / jnp.maximum(pooled_rows, 1.0)[:, None, :], axis=2)


def build_table(totals, zone_rows, zone_share, widths, offsets, day_total):
    zone_terms = jnp.einsum(
        "cr,srb->scb",
        zone_rows,
        zone_share,
        precision=lax.Precision.HIGHEST,
        preferred_element_type=jnp.float32,
    )
    pooled = totals + pool_weight * day_total * zone_terms
    bins_total = pooled.shape[2]
    ladder = jnp.arange(bins_total, dtype=jnp.int32)
    upper_mask = (ladder[:, None] <= ladder[None, :]).astype(jnp.float32)
    running = jnp.einsum(
        "scb,bd->scd",
        pooled,
        upper_mask,
        precision=lax.Precision.HIGHEST,
        preferred_element_type=jnp.float32,
    )
    before = running - pooled
    future_rank = before[2] + 0.5 * pooled[2]
    row_count = pooled.shape[1]
    group_size = math.gcd(row_count, 128)
    group_count = row_count // group_size

    def per_group(group_rows):
        rank_rows, obs_before, obs_pooled, hist_before, hist_pooled = group_rows
        return (
            quantile_at(rank_rows, obs_before, obs_pooled),
            quantile_at(rank_rows, hist_before, hist_pooled),
        )

    shaped = (
        future_rank.reshape(group_count, group_size, bins_total),
        before[1].reshape(group_count, group_size, bins_total),
        pooled[1].reshape(group_count, group_size, bins_total),
        before[0].reshape(group_count, group_size, bins_total),
        pooled[0].reshape(group_count, group_size, bins_total),
    )
    quant_obs, quant_hist = lax.map(per_group, shaped)
    quant_obs = quant_obs.reshape(row_count, bins_total)
    quant_hist = quant_hist.reshape(row_count, bins_total)
    centers = (ladder.astype(jnp.float32) + 0.5)[None, :]
    return offsets[:, None] + widths[:, None] * (centers + quant_obs - quant_hist)


def apply_table(fut_bin, lookup, levels):
    day_count, cell_count = fut_bin.shape
    day_block = math.gcd(day_count, max(1, 16384 // cell_count))
    folded = fut_bin.reshape(day_count // day_block, day_block, cell_count)

    def select_rows(bins_rows):
        matches = bins_rows[..., None] == levels
        return jnp.sum(jnp.where(matches, lookup[None], 0.0), axis=2)

    return lax.map(select_rows, folded).reshape(day_count, cell_count)


def body(hist_bin, obs_bin, fut_bin, region_id, bin_width, bin_offset):
    day_count, cell_count = hist_bin.shape
    levels = jnp.arange(BINS, dtype=jnp.int32)
    stacked = jnp.stack([hist_bin, obs_bin, fut_bin])
    totals = tally_bins(stacked, levels)
    zone_rows = (region_id[:, None] == jnp.arange(REGIONS, dtype=jnp.int32)[None, :]).astype(
        jnp.float32
    )
    zone_part = jnp.einsum(
        "cr,scb->srb",
        zone_rows,
        totals,
        precision=lax.Precision.HIGHEST,
        preferred_element_type=jnp.float32,
    )
    zone_counts = lax.psum(zone_part, ("tm", "cells"))
    zone_share = zone_counts / jnp.sum(zone_counts, axis=2, keepdims=True)
    day_total = day_count * lax.axis_size("tm")
    share_rows = lax.psum_scatter(totals, "tm", scatter_dimension=1, tiled=True)
    share_count = share_rows.shape[1]
    first_row = lax.axis_index("tm") * share_count
    share_zones = lax.dynamic_slice_in_dim(zone_rows, first_row, share_count, 0)
    share_widths = lax.dynamic_slice_in_dim(bin_width, first_row, share_count, 0)
    share_offsets = lax.dynamic_slice_in_dim(bin_offset, first_row, share_count, 0)
    partial_table = build_table(
        share_rows, share_zones, zone_share, share_widths, share_offsets, day_total
    )
    lookup = collect(partial_table, "tm", 0)
    return apply_table(fut_bin, lookup, levels)


def solution(mesh):
    placed = (
        P("tm", "cells"),
        P("tm", "cells"),
        P("tm", "cells"),
        P("cells"),
        P("cells"),
        P("cells"),
    )
    return jax.shard_map(
        body, mesh=mesh, in_specs=placed, out_specs=P("tm", "cells"), check_vma=False
    )
```

profile of v0, /device:TPU:1, one launch (start us, length us, event | category | flops | bytes accessed | tf_op | source)
XLA Modules:
  0.0 995.9 jit_solution(16803068548199994457)
XLA Ops:
  7.4 6.6 pad_add_fusion
  14.0 453.7 %while.31 = (s32[]{:T(128)}, f32[3,1024,256]{2,1,0:T(8,128)}, s32[3,512,1024]{2,1,0:T(8,128)}, s32[]{:T(128)}, s32[]{:T(128)}, /*index=5*/s32[]{:T(128)}, s32[]{:T(128)}) while((s32[]{:T(128)}, f32[3,1024,256]{2,1,0:T(8,128)}, s32[3,512,1024]{2,1,0:T(8,128)}, s32[]{:T(128)}, s32[]{:T(128)}, /*index=5*/s32[]{:T(128)}, ...), condition=%wide.region_2.0_spmd.clone, body=%wide.region_0.0_spmd.clone.sunk | while | flops 51118084 | bytes 13172873 | solution.py:39
  15.0 9.3 convert_reduce_fusion.2
  27.3 9.3 convert_reduce_fusion.2
  41.6 9.3 convert_reduce_fusion.2
  55.8 9.3 convert_reduce_fusion.2
  70.0 9.3 convert_reduce_fusion.2
  84.3 9.3 convert_reduce_fusion.2
  98.5 9.3 convert_reduce_fusion.2
  112.7 9.3 convert_reduce_fusion.2
  127.0 9.3 convert_reduce_fusion.2
  141.2 9.3 convert_reduce_fusion.2
  155.5 9.3 convert_reduce_fusion.2
  169.7 9.3 convert_reduce_fusion.2
  183.9 9.3 convert_reduce_fusion.2
  198.2 9.3 convert_reduce_fusion.2
  212.4 9.3 convert_reduce_fusion.2
  226.6 9.3 convert_reduce_fusion.2
  240.9 9.3 convert_reduce_fusion.2
  255.1 9.3 convert_reduce_fusion.2
  269.4 9.3 convert_reduce_fusion.2
  283.6 9.3 convert_reduce_fusion.2
  297.8 9.3 convert_reduce_fusion.2
  312.1 9.3 convert_reduce_fusion.2
  326.3 9.3 convert_reduce_fusion.2
  340.5 9.3 convert_reduce_fusion.2
  354.8 9.3 convert_reduce_fusion.2
  369.0 9.3 convert_reduce_fusion.2
  383.2 9.3 convert_reduce_fusion.2
  397.5 9.3 convert_reduce_fusion.2
  411.7 9.3 convert_reduce_fusion.2
  426.0 9.3 convert_reduce_fusion.2
  440.2 9.3 convert_reduce_fusion.2
  454.4 9.3 convert_reduce_fusion.2
  467.7 5.4 convolution_bitcast_fusion
  475.5 253.2 %all-reduce.2.cloned.1.call-done = f32[3,128,256]{1,2,0:T(8,128)} async-done(((f32[3,128,256]{1,2,0:T(8,128)}), f32[3,128,256]{1,2,0:T(8,128)}) %all-reduce.2.cloned.1.call-update) | async-done | bytes 393232 | tf_op jit(solution)/shard_map/psum | solution.py:122
  736.6 6.3 all-to-all-start
  742.8 26.6 %all-to-all-done = f32[32,32,256]{2,1,0:T(8,128)S(1)} async-done(((f32[32,32,256]{2,1,0:T(8,128)}), f32[32,32,256]{2,1,0:T(8,128)S(1)}, u32[]{:S(2)}, u32[]{:S(2)}) %all-to-all-start) | async-done | bytes 1048608 | tf_op jit(solution)/shard_map/all_to_all | solution.py:20
  769.5 219.0 %while.30 = (s32[]{:T(128)}, f32[32,16,1024]{2,1,0:T(8,128)}, s32[32,16,1024]{2,1,0:T(8,128)}, f32[32,32,256]{2,1,0:T(8,128)S(1)}, s32[]{:T(128)}) while((s32[]{:T(128)}, f32[32,16,1024]{2,1,0:T(8,128)}, s32[32,16,1024]{2,1,0:T(8,128)}, f32[32,32,256]{2,1,0:T(8,128)S(1)}, s32[]{:T(128)}) %tuple.66), condition=%wide.region_10.11_spmd.clone, body=%wide.region_8.10_spmd.clone.sunk | while | flops 12566530 | bytes 1442369 | solution.py:104
  770.3 5.3 select_reduce_fusion.2
  777.2 5.3 select_reduce_fusion.2
  784.0 5.3 select_reduce_fusion.2
  790.8 5.3 select_reduce_fusion.2
  797.7 5.3 select_reduce_fusion.2
  804.5 5.3 select_reduce_fusion.2
  811.4 5.3 select_reduce_fusion.2
  818.2 5.3 select_reduce_fusion.2
  825.1 5.3 select_reduce_fusion.2
  831.9 5.3 select_reduce_fusion.2
  838.8 5.3 select_reduce_fusion.2
  845.6 5.3 select_reduce_fusion.2
  852.4 5.3 select_reduce_fusion.2
  859.3 5.3 select_reduce_fusion.2
  866.1 5.3 select_reduce_fusion.2
  873.0 5.3 select_reduce_fusion.2
  879.8 5.3 select_reduce_fusion.2
  886.7 5.3 select_reduce_fusion.2
  893.5 5.3 select_reduce_fusion.2
  900.3 5.3 select_reduce_fusion.2
  907.2 5.3 select_reduce_fusion.2
  914.0 5.3 select_reduce_fusion.2
  920.9 5.3 select_reduce_fusion.2
  927.7 5.3 select_reduce_fusion.2
  934.6 5.3 select_reduce_fusion.2
  (156 shorter events, 251.4 us)
Async XLA Ops:
  7.4 721.3 %all-reduce.2.cloned.1.call-start = ((), (), s32[]{:S(2)}) async-start(), calls=%async_computation.3 | async-start | bytes 786432 | tf_op jit(solution)/shard_map/psum | solution.py:122
  14.0 453.7 %copy-start = (s32[1024]{0:T(1024)S(1)}, s32[1024]{0:T(1024)}, u32[]{:S(2)}) copy-start(s32[1024]{0:T(1024)} %param.13) | copy-start | bytes 12292
  473.2 256.6 %reduce-scatter.2.cloned.1.call-start = ((), (), s32[]{:S(2)}) async-start(), calls=%async_computation.2 | async-start | bytes 3244032 | tf_op jit(solution)/shard_map/reduce_scatter | solution.py:125
  736.6 32.9 %all-to-all-start = ((f32[32,32,256]{2,1,0:T(8,128)}), f32[32,32,256]{2,1,0:T(8,128)S(1)}, u32[]{:S(2)}, u32[]{:S(2)}) async-start(f32[32,32,256]{2,1,0:T(8,128)} %broadcast_in_dim.68), calls=%async_computation.1 | async-start | bytes 2097152 | tf_op jit(solution)/shard_map/all_to_all | solution.py:20
Sparse Core Ops, SparseCore 0:
  473.3 255.3 all-reduce.1
Sparse Core Ops, SparseCore 1:
  476.2 149.1 reduce-scatter.1
where the time goes:
time: 1000 us; the launch traced here: 996 us
  other arithmetic  606 us (61%)
  waiting for transfers between devices  280 us (28%)
  local copies, waits for them, and re-layouts  80.2 us (8%)
  between operations  14.9 us (1%)
    reduce_sum x32, other arithmetic, add_block(): return totals + jnp.sum(matches, axis=1, dtype=jnp.float32)  297 us
    psum x1, waiting for transfers between devices, body(): zone_counts = lax.psum(zone_part, ('tm', 'cells'))  253 us
    reduce_sum x32, other arithmetic, select_rows(): return jnp.sum(jnp.where(matches, lookup[None], 0.0), axis=2)  171 us
    add x32, other arithmetic, add_block(): return totals + jnp.sum(matches, axis=1, dtype=jnp.float32)  126 us
    dynamic_slice x32, local copies, waits for them, and re-layouts, add_block(): lax.dynamic_slice_in_dim(stacked, turn_index * day_block, day_block, 1)  30.1 us
    eq x32, local copies, waits for them, and re-layouts, select_rows(): matches = bins_rows[..., None] == levels  27 us
    all_to_all x1, waiting for transfers between devices, copy_for_each(): lax.all_to_all(jnp.broadcast_to(array[None], (count, *array.shape)), axis...  26.6 us
    dynamic_update_slice x32, local copies, waits for them, and re-layouts, apply_table(): return lax.map(select_rows, folded).reshape(day_count, cell_count)  20.5 us
  transfers between devices with their start and end apart: 3, of which 2 were waited for; matrix products, arithmetic and copies ran while one was open for 0% of the time, Pallas kernels for 0%

commit v1 on v0

--- a/solution.py
+++ b/solution.py
@@ -119,7 +119,7 @@
         precision=lax.Precision.HIGHEST,
         preferred_element_type=jnp.float32,
     )
-    zone_counts = lax.psum(zone_part, ("tm", "cells"))
+    zone_counts = lax.psum(lax.psum(zone_part, "tm"), "cells")
     zone_share = zone_counts / jnp.sum(zone_counts, axis=2, keepdims=True)
     day_total = day_count * lax.axis_size("tm")
     share_rows = lax.psum_scatter(totals, "tm", scatter_dimension=1, tiled=True)

time: 1000 us -> 1280 us (1.28)
  waiting for transfers between devices: 280 us -> 550 us
    reduce_scatter x1, waiting for transfers between devices: 0.02 us -> 147 us  [body(): share_rows = lax.psum_scatter(totals, 'tm', scatter_dimension=1, tiled=True)]
    psum x1 -> x2, waiting for transfers between devices: 253 us -> 375 us  [body(): zone_counts = lax.psum(lax.psum(zone_part, 'tm'), 'cells')]
  transfers between devices with their start and end apart: 3 -> 4, of which waited for: 2 -> 4; matrix products, arithmetic and copies ran while one was open for 0% -> 0% of each run, Pallas kernels for 0% -> 0%
where the time goes in v1:
time: 1280 us; the launch traced here: 1270 us
  other arithmetic  613 us (48%)
  waiting for transfers between devices  550 us (43%)
  local copies, waits for them, and re-layouts  80.2 us (6%)
  between operations  13.2 us (1%)
    psum x2, waiting for transfers between devices, body(): zone_counts = lax.psum(lax.psum(zone_part, 'tm'), 'cells')  375 us
    reduce_sum x32, other arithmetic, add_block(): return totals + jnp.sum(matches, axis=1, dtype=jnp.float32)  297 us
    reduce_sum x32, other arithmetic, select_rows(): return jnp.sum(jnp.where(matches, lookup[None], 0.0), axis=2)  171 us
    reduce_scatter x1, waiting for transfers between devices, body(): share_rows = lax.psum_scatter(totals, 'tm', scatter_dimension=1, tiled=True)  147 us
    add x32, other arithmetic, add_block(): return totals + jnp.sum(matches, axis=1, dtype=jnp.float32)  133 us
    dynamic_slice x32, local copies, waits for them, and re-layouts, add_block(): lax.dynamic_slice_in_dim(stacked, turn_index * day_block, day_block, 1)  30.1 us
    eq x32, local copies, waits for them, and re-layouts, select_rows(): matches = bins_rows[..., None] == levels  27 us
    all_to_all x1, waiting for transfers between devices, copy_for_each(): lax.all_to_all(jnp.broadcast_to(array[None], (count, *array.shape)), axis...  26.8 us
  transfers between devices with their start and end apart: 4, of which 4 were waited for; matrix products, arithmetic and copies ran while one was open for 0% of the time, Pallas kernels for 0%

profile of v1, /device:TPU:1, one launch (start us, length us, event | category | flops | bytes accessed | tf_op | source)
XLA Modules:
  0.0 1273.0 jit_solution(15690752508557590470)
XLA Ops:
  6.5 6.6 pad_add_fusion
  13.2 460.2 %while.31 = (s32[]{:T(128)}, f32[3,1024,256]{2,1,0:T(8,128)}, s32[3,512,1024]{2,1,0:T(8,128)}, s32[]{:T(128)}, s32[]{:T(128)}, /*index=5*/s32[]{:T(128)}, s32[]{:T(128)}) while((s32[]{:T(128)}, f32[3,1024,256]{2,1,0:T(8,128)}, s32[3,512,1024]{2,1,0:T(8,128)}, s32[]{:T(128)}, s32[]{:T(128)}, /*index=5*/s32[]{:T(128)}, ...), condition=%wide.region_2.0_spmd.clone, body=%wide.region_0.0_spmd.clone.sunk | while | flops 51118084 | bytes 13172873 | solution.py:39
  14.1 9.3 convert_reduce_fusion.2
  26.7 9.3 convert_reduce_fusion.2
  41.1 9.3 convert_reduce_fusion.2
  55.6 9.3 convert_reduce_fusion.2
  70.0 9.3 convert_reduce_fusion.2
  84.4 9.3 convert_reduce_fusion.2
  98.9 9.3 convert_reduce_fusion.2
  113.3 9.3 convert_reduce_fusion.2
  127.8 9.3 convert_reduce_fusion.2
  142.2 9.3 convert_reduce_fusion.2
  156.6 9.3 convert_reduce_fusion.2
  171.1 9.3 convert_reduce_fusion.2
  185.5 9.3 convert_reduce_fusion.2
  200.0 9.3 convert_reduce_fusion.2
  214.4 9.3 convert_reduce_fusion.2
  228.8 9.3 convert_reduce_fusion.2
  243.3 9.3 convert_reduce_fusion.2
  257.7 9.3 convert_reduce_fusion.2
  272.1 9.3 convert_reduce_fusion.2
  286.6 9.3 convert_reduce_fusion.2
  301.0 9.3 convert_reduce_fusion.2
  315.5 9.3 convert_reduce_fusion.2
  329.9 9.3 convert_reduce_fusion.2
  344.3 9.3 convert_reduce_fusion.2
  358.8 9.3 convert_reduce_fusion.2
  373.2 9.3 convert_reduce_fusion.2
  387.7 9.3 convert_reduce_fusion.2
  402.1 9.3 convert_reduce_fusion.2
  416.5 9.3 convert_reduce_fusion.2
  431.0 9.3 convert_reduce_fusion.2
  445.4 9.3 convert_reduce_fusion.2
  459.8 9.3 convert_reduce_fusion.2
  473.3 5.4 convolution_bitcast_fusion
  478.8 270.5 %all-reduce.3.cloned.1.call-done = f32[3,128,256]{1,2,0:T(8,128)} async-done(((f32[3,128,256]{1,2,0:T(8,128)}), f32[3,128,256]{1,2,0:T(8,128)}) %all-reduce.3.cloned.1.call-update) | async-done | bytes 393232 | tf_op jit(solution)/shard_map/psum | solution.py:122
  751.8 105.0 %all-reduce.5.cloned.1.call-done = f32[3,128,256]{1,2,0:T(8,128)} async-done(((f32[3,128,256]{1,2,0:T(8,128)}), f32[3,128,256]{1,2,0:T(8,128)}) %all-reduce.5.cloned.1.call-update) | async-done | bytes 393232 | tf_op jit(solution)/shard_map/psum | solution.py:122
  857.8 146.6 %reduce-scatter.2.cloned.1.call-done = f32[3,32,256]{2,1,0:T(8,128)} async-done(((f32[3,1024,256]{2,1,0:T(8,128)}), f32[3,32,256]{2,1,0:T(8,128)}) %reduce-scatter.2.cloned.1.call-update) | async-done | bytes 98320 | tf_op jit(solution)/shard_map/reduce_scatter | solution.py:125
  1011.2 9.4 all-to-all-start
  1020.7 26.8 %all-to-all-done = f32[32,32,256]{2,1,0:T(8,128)S(1)} async-done(((f32[32,32,256]{2,1,0:T(8,128)}), f32[32,32,256]{2,1,0:T(8,128)S(1)}, u32[]{:S(2)}, u32[]{:S(2)}) %all-to-all-start) | async-done | bytes 1048608 | tf_op jit(solution)/shard_map/all_to_all | solution.py:20
  1047.4 219.0 %while.30 = (s32[]{:T(128)}, f32[32,16,1024]{2,1,0:T(8,128)}, s32[32,16,1024]{2,1,0:T(8,128)}, f32[32,32,256]{2,1,0:T(8,128)S(1)}, s32[]{:T(128)}) while((s32[]{:T(128)}, f32[32,16,1024]{2,1,0:T(8,128)}, s32[32,16,1024]{2,1,0:T(8,128)}, f32[32,32,256]{2,1,0:T(8,128)S(1)}, s32[]{:T(128)}) %tuple.68), condition=%wide.region_11.12_spmd.clone, body=%wide.region_9.11_spmd.clone.sunk | while | flops 12566530 | bytes 1442369 | solution.py:104
  1048.3 5.3 select_reduce_fusion.2
  1055.1 5.3 select_reduce_fusion.2
  1062.0 5.3 select_reduce_fusion.2
  1068.8 5.3 select_reduce_fusion.2
  1075.7 5.3 select_reduce_fusion.2
  1082.5 5.3 select_reduce_fusion.2
  1089.3 5.3 select_reduce_fusion.2
  1096.2 5.3 select_reduce_fusion.2
  1103.0 5.3 select_reduce_fusion.2
  1109.9 5.3 select_reduce_fusion.2
  1116.7 5.3 select_reduce_fusion.2
  1123.6 5.3 select_reduce_fusion.2
  1130.4 5.3 select_reduce_fusion.2
  1137.2 5.3 select_reduce_fusion.2
  1144.1 5.3 select_reduce_fusion.2
  1150.9 5.3 select_reduce_fusion.2
  1157.8 5.3 select_reduce_fusion.2
  1164.6 5.3 select_reduce_fusion.2
  1171.5 5.3 select_reduce_fusion.2
  1178.3 5.3 select_reduce_fusion.2
  1185.2 5.3 select_reduce_fusion.2
  1192.0 5.3 select_reduce_fusion.2
  1198.8 5.3 select_reduce_fusion.2
  (159 shorter events, 268.7 us)
Async XLA Ops:
  6.5 742.7 %all-reduce.3.cloned.1.call-start = ((), (), s32[]{:S(2)}) async-start(), calls=%async_computation.3 | async-start | bytes 786432 | tf_op jit(solution)/shard_map/psum | solution.py:122
  13.2 460.2 %copy-start = (s32[1024]{0:T(1024)S(1)}, s32[1024]{0:T(1024)}, u32[]{:S(2)}) copy-start(s32[1024]{0:T(1024)} %param.13) | copy-start | bytes 12292
  478.8 378.0 %all-reduce.5.cloned.1.call-start = ((), (), s32[]{:S(2)}) async-start(), calls=%async_computation.4 | async-start | bytes 786432 | tf_op jit(solution)/shard_map/psum | solution.py:122
  749.3 255.1 %reduce-scatter.2.cloned.1.call-start = ((), (), s32[]{:S(2)}) async-start(), calls=%async_computation.2 | async-start | bytes 3244032 | tf_op jit(solution)/shard_map/reduce_scatter | solution.py:125
  1011.2 36.2 %all-to-all-start = ((f32[32,32,256]{2,1,0:T(8,128)}), f32[32,32,256]{2,1,0:T(8,128)S(1)}, u32[]{:S(2)}, u32[]{:S(2)}) async-start(f32[32,32,256]{2,1,0:T(8,128)} %broadcast_in_dim.68), calls=%async_computation.1 | async-start | bytes 2097152 | tf_op jit(solution)/shard_map/all_to_all | solution.py:20
Sparse Core Ops, SparseCore 0:
  478.9 270.3 all-reduce.2
  751.9 104.8 all-reduce.4
  859.3 145.0 reduce-scatter.1
